TPU v7x, 256 devices: a whole 4x4x8 slice. The times are simulated.
256 devices in a mesh: gx: 16 (over x_lo, z), ma: 16 (over y, x_hi, core).
Axes of the slice: x: 4 (x_hi: 2, x_lo: 2; x = x_hi * 2 + x_lo), y: 4, z: 8, core: 2. Of those that a mesh axis runs over, the one named last changes fastest.
Arguments:
- solution: float32 [256, 16, 8, 256], P('ma', 'gx'), may hold values from -1.2 to 1.2
- source: float32 [256, 16, 8, 256], P('ma', 'gx'), may hold values from -6 to 6
- mean_conductivity: float32 [16, 8, 256], P('gx'), may hold values from 0.5 to 2
- kl_fields: float32 [10, 16, 8, 256], P(None, 'gx'), may hold values from -0.9 to 0.9
- couplings: int32 [10, 256, 2], replicated, may hold values from 0 to 255, as said below
- mode_index: int32 [256, 10], replicated, may hold values from 0 to 3, as said below
Outputs:
- residual: float32 [256, 16, 8, 256], P('ma', 'gx')
- correction: float32 [256, 16, 8, 256], P('ma', 'gx')
Inputs may be any that keep to these rules, and one draw needn't show every extreme that they name: couplings[k, i, 0] is the mode whose multi-index is mode_index[i] plus one in variable k, couplings[k, i, 1] the mode whose multi-index is mode_index[i] minus one in variable k; where no mode has that multi-index the entry is i itself. `mode_index`: the rows are 256 distinct multi-indices of total degree at most 3 in graded order: the total degree never falls with the mode number, all multi-indices of each total degree below 3 are present, and some mode has degree 3 in one variable; the order of the variables is drawn from the seed.
All inputs are finite; a program needn't handle non-finite values.
Results may differ from a plain program's by a relative error of at most 0.000071.
Values sent between devices are 32-bit elements; how exact they have to be, the bound alone decides.
No kernel may reach another device: no remote copies, remote signals or barrier semaphores. Data moves between devices by JAX's collectives and lax.ppermute only.
A program may use at most 128 MiB of HBM per device.

v0:
```python
import jax
import jax.numpy as jnp
from jax import lax
from jax.sharding import PartitionSpec as P

STEPS = 3


def extended(array, sides, width):
    for axis, dim in sides:
        size, length = (lax.axis_size(axis), array.shape[dim])
        up = [(i, (i + 1) % size) for i in range(size)]
        down = [(j, i) for i, j in up]
        last = lax.slice_in_dim(array, length - width, length, axis=dim)
        initial = lax.slice_in_dim(array, 0, width, axis=dim)
        before = lax.ppermute(last, axis, up)
        after = lax.ppermute(initial, axis, down)
        array = jnp.concatenate([before, array, after], axis=dim)
    return array


def diffuse(coefficient, padded):
    center = coefficient[1:-1]
    values = padded[..., 1:-1, :, :]
    total = 0.5 * (center + coefficient[2:]) * (values - padded[..., 2:, :, :])
    total = total + 0.5 * (center + coefficient[:-2]) * (values - padded[..., :-2, :, :])
    for which_dim in (-2, -1):
        for offset in (-1, 1):
            total = total + 0.5 * (center + jnp.roll(center, offset, which_dim)) * (
                values - jnp.roll(values, offset, which_dim)
            )
    return total


def coupling_table(couplings, mode_index):
    modes_all = mode_index.shape[0]
    degrees = mode_index.astype(jnp.float32).T
    weight = jnp.sqrt(jnp.maximum(degrees[:, :, None], degrees[:, None, :]))
    columns = lax.broadcasted_iota(jnp.int32, (1, 1, 1, modes_all), 3)
    counted = jnp.sum((couplings[..., None] == columns).astype(jnp.float32), axis=2)
    row_ids = lax.broadcasted_iota(jnp.int32, (1, modes_all, modes_all), 1)
    col_ids = lax.broadcasted_iota(jnp.int32, (1, modes_all, modes_all), 2)
    off_diagonal = (row_ids != col_ids).astype(jnp.float32)
    return counted * weight * off_diagonal


def shards(solution, source, mean_conductivity, kl_fields, couplings, mode_index):
    modes_here = solution.shape[0]
    fields = kl_fields.shape[0]
    shape = solution.shape
    cells = shape[1] * shape[2] * shape[3]
    block_start = lax.axis_index("ma") * modes_here
    g_full = coupling_table(couplings, mode_index)
    g_rows = lax.dynamic_slice_in_dim(g_full, block_start, modes_here, 1)
    stacked = jnp.concatenate([mean_conductivity[None], kl_fields], 0)
    padded_fields = extended(stacked, (("gx", 1),), 1)
    mean_pad = padded_fields[0]
    kl_pad = padded_fields[1:]
    padded_solution = extended(solution, (("gx", 1),), 1)
    image = solution + diffuse(mean_pad, padded_solution)
    piece = lax.all_gather(padded_solution, "ma", axis=0, tiled=True)
    count = piece.shape[0]
    terms = jnp.stack([diffuse(kl_pad[field_id], piece) for field_id in range(fields)])
    terms = terms.reshape(fields, count, cells)
    coupled = jnp.einsum("kij,kjc->ic", g_rows, terms, precision=lax.Precision.HIGHEST)
    image = image + coupled.reshape(shape)
    residual = source - image
    theta = 13.0
    delta = 12.0
    sigma = theta / delta
    rho = 1.0 / sigma
    direction = residual / theta
    correction = direction
    remain = residual
    for step in range(STEPS):
        padded_direction = extended(direction, (("gx", 1),), 1)
        applied = direction + diffuse(mean_pad, padded_direction)
        remain = remain - applied
        rho_next = 1.0 / (2.0 * sigma - rho)
        direction = rho_next * rho * direction + 2.0 * rho_next / delta * remain
        correction = correction + direction
        rho = rho_next
    return (residual, correction)


def solution(mesh):
    in_specs = (
        P("ma", "gx", None, None),
        P("ma", "gx", None, None),
        P("gx", None, None),
        P(None, "gx", None, None),
        P(),
        P(),
    )
    out_specs = (P("ma", "gx", None, None), P("ma", "gx", None, None))
    return jax.shard_map(shards, mesh=mesh, in_specs=in_specs, out_specs=out_specs, check_vma=False)
```

profile of v0, /device:TPU:2, one launch (start us, length us, event | category | flops | bytes accessed | tf_op | source)
XLA Modules:
  0.0 236.9 jit_solution(6606500784124083350)
XLA Ops:
  7.2 1.0 copy.125
  8.2 5.9 %collective-permute-start.1 = (f32[16,1,8,256]{3,0,2,1:T(8,128)S(1)}, f32[16,1,8,256]{3,0,2,1:T(8,128)S(1)}, u32[]{:S(2)}, u32[]{:S(2)}) collective-permute-start(f32[16,1,8,256]{3,0,2,1:T(8,128)S(1)} %copy.125), channel_id=1, source_target_pairs={{16,0},{32,16},{48,32},{64,48},{80,64},{96,80},{112,96},{128,112},... | collective-permute-start | bytes 393224 | tf_op jit(solution)/shard_map/ppermute | solution.py:17
  14.1 2.8 %collective-permute-done.1 = f32[16,1,8,256]{3,0,2,1:T(8,128)S(1)} collective-permute-done((f32[16,1,8,256]{3,0,2,1:T(8,128)S(1)}, f32[16,1,8,256]{3,0,2,1:T(8,128)S(1)}, u32[]{:S(2)}, u32[]{:S(2)}) %collective-permute-start.1) | collective-permute-done | bytes 131104 | tf_op jit(solution)/shard_map/ppermute | solution.py:17
  16.9 4.3 %collective-permute-done.3 = f32[16,1,8,256]{3,0,2,1:T(8,128)S(1)} collective-permute-done((f32[16,1,8,256]{3,0,2,1:T(8,128)S(1)}, f32[16,1,8,256]{3,0,2,1:T(8,128)S(1)}, u32[]{:S(2)}, u32[]{:S(2)}) %collective-permute-start.3) | collective-permute-done | bytes 131104 | tf_op jit(solution)/shard_map/ppermute | solution.py:16
  22.0 0.9 pad_maximum_fusion.1
  23.2 1.8 collective-permute-start.2
  25.6 4.0 %convert_reduce_fusion = f32[10,256,256]{2,1,0:T(8,128)} fusion(s32[10,256,2]{1,2,0:T(2,128)} %param.10), kind=kLoop, calls=%fused_computation | loop fusion | flops 3276800 | bytes 2641920 | tf_op jit(solution)/shard_map/reduce_sum | solution.py:40
  41.9 45.2 %all-gather.2.cloned.1.call-done = f32[256,3,8,256]{3,0,2,1:T(8,128)} async-done(((f32[16,3,8,256]{3,0,2,1:T(8,128)}), f32[256,3,8,256]{3,0,2,1:T(8,128)}) %all-gather.2.cloned.1.call-update) | async-done | bytes 6291472 | tf_op jit(solution)/shard_map/all_gather | solution.py:61
  87.1 4.4 %fusion.185 = (f32[256,1,8,255]{3,0,2,1:T(8,128)S(1)}, f32[256,1,8,255]{3,0,2,1:T(8,128)}) fusion(f32[256,3,8,256]{3,0,2,1:T(8,128)} %all-gather.2.cloned.1.call-done), kind=kLoop, calls=%fused_computation.401 | loop fusion | bytes 8355840 | tf_op jit(solution)/shard_map/jit(_roll_static)/slice | solution.py:30
  91.5 2.2 fusion.187
  94.6 5.4 %multiply_add_fusion = (f32[256,1,8,256]{3,0,2,1:T(8,128)}, f32[256,1,8,256]{3,0,2,1:T(8,128)S(1)}, f32[256,1,8,256]{3,0,2,1:T(8,128)S(1)}, f32[256,1,8,256]{3,0...) fusion(f32[8,256]{1,0:T(8,128)S(1)} %copy-done.93, ...), kind=kLoop, calls=%fused_computation.8 | loop fusion | flops 11010048 | bytes 29409280 | tf_op jit(solution)/shard_map/add | solution.py:29
  100.1 4.4 %multiply_add_fusion.1 = (f32[256,1,8,256]{3,0,2,1:T(8,128)}, f32[256,1,8,256]{3,0,2,1:T(8,128)}) fusion(f32[256,1,8,256]{3,0,2,1:T(8,128)S(1)} %get-tuple-element.18, f32[256,1,8,256]{3,0,2,1:T(8,128)S(1)} %get-tuple-element.17, f32[256,1,8,256]{3,0,2,1:T(8,128)S(1)} %get-tuple-element.16, f32[256,1,8,256]{3,0,2,1:T(8,128)S(1)} %get-tuple-element.15, ...), kind=kLoop, calls=%fused_computation.9 | loop fusion | flops 11534336 | bytes 16875520 | tf_op jit(solution)/shard_map/add | solution.py:29
  105.2 3.1 %copy.150 = f32[256,1,8,256]{0,3,2,1:T(8,128)} copy(f32[256,1,8,256]{3,0,2,1:T(8,128)} %get-tuple-element.20) | data formatting | bytes 4194304 | tf_op jit(solution)/shard_map/add | solution.py:29
  108.4 6.5 %multiply_add_fusion.3 = (f32[256,1,8,256]{3,0,2,1:T(8,128)}, f32[256,1,8,256]{3,0,2,1:T(8,128)}) fusion(f32[256,1,8,256]{3,0,2,1:T(8,128)} %copy-done.4, f32[256,1,8,256]{3,0,2,1:T(8,128)} %copy-done.3, f32[256,1,8,256]{3,0,2,1:T(8,128)} %copy-done.2, f32[256,1,8,256]{3,0,2,1:T(8,128)} %copy-done.1, f32[256,1,8,256]{3,0,2,1:T(8,128)} %copy-done, ...), kind=kLoop, calls=%fused_computation.11 | loop fusion | flops 11534336 | bytes 16875520 | tf_op jit(solution)/shard_map/add | solution.py:29
  115.0 3.0 %copy.144 = f32[256,1,8,256]{0,3,2,1:T(8,128)} copy(f32[256,1,8,256]{3,0,2,1:T(8,128)} %get-tuple-element.22) | data formatting | bytes 4194304 | tf_op jit(solution)/shard_map/add | solution.py:29
  118.1 6.5 %multiply_add_fusion.5 = (f32[256,1,8,256]{3,0,2,1:T(8,128)}, f32[256,1,8,256]{3,0,2,1:T(8,128)}) fusion(f32[256,1,8,256]{3,0,2,1:T(8,128)} %copy-done.4, f32[256,1,8,256]{3,0,2,1:T(8,128)} %copy-done.3, f32[256,1,8,256]{3,0,2,1:T(8,128)} %copy-done.2, f32[256,1,8,256]{3,0,2,1:T(8,128)} %copy-done.1, f32[256,1,8,256]{3,0,2,1:T(8,128)} %copy-done, ...), kind=kLoop, calls=%fused_computation.13 | loop fusion | flops 11534336 | bytes 16875520 | tf_op jit(solution)/shard_map/add | solution.py:29
  124.7 3.0 %copy.138 = f32[256,1,8,256]{0,3,2,1:T(8,128)} copy(f32[256,1,8,256]{3,0,2,1:T(8,128)} %get-tuple-element.24) | data formatting | bytes 4194304 | tf_op jit(solution)/shard_map/add | solution.py:29
  127.8 6.5 %multiply_add_fusion.7 = (f32[256,1,8,256]{3,0,2,1:T(8,128)}, f32[256,1,8,256]{3,0,2,1:T(8,128)}) fusion(f32[256,1,8,256]{3,0,2,1:T(8,128)} %copy-done.4, f32[256,1,8,256]{3,0,2,1:T(8,128)} %copy-done.3, f32[256,1,8,256]{3,0,2,1:T(8,128)} %copy-done.2, f32[256,1,8,256]{3,0,2,1:T(8,128)} %copy-done.1, f32[256,1,8,256]{3,0,2,1:T(8,128)} %copy-done, ...), kind=kLoop, calls=%fused_computation.15 | loop fusion | flops 11534336 | bytes 16875520 | tf_op jit(solution)/shard_map/add | solution.py:29
  134.3 3.0 %copy.132 = f32[256,1,8,256]{0,3,2,1:T(8,128)} copy(f32[256,1,8,256]{3,0,2,1:T(8,128)} %get-tuple-element.26) | data formatting | bytes 4194304 | tf_op jit(solution)/shard_map/add | solution.py:29
  137.3 6.7 %multiply_add_fusion.9 = f32[256,1,8,256]{3,0,2,1:T(8,128)} fusion(f32[256,1,8,256]{3,0,2,1:T(8,128)} %copy-done.4, f32[256,1,8,256]{3,0,2,1:T(8,128)} %copy-done.3, f32[256,1,8,256]{3,0,2,1:T(8,128)} %copy-done.2, f32[256,1,8,256]{3,0,2,1:T(8,128)} %copy-done.1, f32[256,1,8,256]{3,0,2,1:T(8,128)} %copy-done, f32[256,1,8,256]{3,0,2,1:T(8,128)S(1)} %get-tuple-element.13, ...), kind=kLoop, calls=%fused_computation.17 | loop fusion | flops 5767168 | bytes 14729216 | tf_op jit(solution)/shard_map/add | solution.py:29
  144.1 1.9 copy.129
  146.0 1.5 constant_dynamic-update-slice_fusion.9
  147.5 2.9 %copy.135 = f32[256,1,8,256]{0,3,2,1:T(8,128)} copy(f32[256,1,8,256]{3,0,2,1:T(8,128)} %get-tuple-element.25) | data formatting | bytes 4194304 | tf_op jit(solution)/shard_map/add | solution.py:29
  150.4 3.0 %copy.141 = f32[256,1,8,256]{0,3,2,1:T(8,128)} copy(f32[256,1,8,256]{3,0,2,1:T(8,128)} %get-tuple-element.23) | data formatting | bytes 4194304 | tf_op jit(solution)/shard_map/add | solution.py:29
  153.4 1.8 copy.147
  155.3 3.0 %copy.153 = f32[256,1,8,256]{0,3,2,1:T(8,128)} copy(f32[256,1,8,256]{3,0,2,1:T(8,128)} %get-tuple-element.19) | data formatting | bytes 4194304 | tf_op jit(solution)/shard_map/add | solution.py:29
  158.3 1.8 copy.156
  160.1 3.2 %constant_dynamic-update-slice_fusion.8 = f32[10,256,2048]{1,2,0:T(8,128)} fusion(f32[10,256,2048]{1,2,0:T(8,128)} %constant_dynamic-update-slice_fusion.9, f32[1,256,2048]{1,2,0:T(8,128)} %bitcast.365), kind=kLoop, calls=%fused_computation.102 | loop fusion | bytes 4194304
  163.4 1.5 constant_dynamic-update-slice_fusion.7
  165.7 1.5 constant_dynamic-update-slice_fusion.6
  168.1 1.5 constant_dynamic-update-slice_fusion.5
  170.4 1.4 constant_dynamic-update-slice_fusion.4
  171.8 0.9 copy-done.12
  172.8 1.4 constant_dynamic-update-slice_fusion.3
  174.2 0.9 copy-done.7
  175.1 1.5 constant_dynamic-update-slice_fusion.2
  177.4 1.5 constant_dynamic-update-slice_fusion.1
  179.9 1.5 constant_dynamic-update-slice_fusion
  181.6 20.3 %broadcast_multiply_fusion = (f32[16,1,8,256]{3,0,2,1:T(8,128)S(1)}, f32[16,1,8,256]{3,0,2,1:T(8,128)S(1)}) fusion(f32[8,256,256,10]{2,1,0,3:T(8,128)} %bitcast.361, f32[10,256,256]{2,1,0:T(8,128)} %convert_reduce_fusion, s32[]{:T(128)S(6)} %select_n.3, f32[16,256]{1,0:T(8,128)S(1)} %copy-done.31, f32[10,256]{1,0:T(8,128)S(1)} %copy-done.30, ...), kind=kOutput, calls=%fused_computation.93 | convolution fusion | flops 1007575040 | bytes 22522500 | tf_op jit(solution)/shard_map/kij,kjc->ic/dot_general | solution.py:65
  202.0 4.3 %collective-permute-start.4 = (f32[16,1,8,256]{3,0,2,1:T(8,128)S(1)}, f32[16,1,8,256]{3,0,2,1:T(8,128)S(1)}, u32[]{:S(2)}, u32[]{:S(2)}) collective-permute-start(f32[16,1,8,256]{3,0,2,1:T(8,128)S(1)} %get-tuple-element.232), channel_id=1, source_target_pairs={{16,0},{32,16},{48,32},{64,48},{80,64},{96,80},{112,96},{128,112},... | collective-permute-start | bytes 393224 | tf_op jit(solution)/shard_map/ppermute | solution.py:17
  207.1 2.3 collective-permute-done.4
  209.4 4.3 %collective-permute-done.5 = f32[16,1,8,256]{3,0,2,1:T(8,128)S(1)} collective-permute-done((f32[16,1,8,256]{3,0,2,1:T(8,128)S(1)}, f32[16,1,8,256]{3,0,2,1:T(8,128)S(1)}, u32[]{:S(2)}, u32[]{:S(2)}) %collective-permute-start.5) | collective-permute-done | bytes 131104 | tf_op jit(solution)/shard_map/ppermute | solution.py:16
  214.4 1.7 collective-permute-start.7
  216.3 2.9 %collective-permute-done.6 = f32[16,1,8,256]{3,0,2,1:T(8,128)S(1)} collective-permute-done((f32[16,1,8,256]{3,0,2,1:T(8,128)S(1)}, f32[16,1,8,256]{3,0,2,1:T(8,128)S(1)}, u32[]{:S(2)}, u32[]{:S(2)}) %collective-permute-start.6) | collective-permute-done | bytes 131104 | tf_op jit(solution)/shard_map/ppermute | solution.py:17
  219.1 2.4 %collective-permute-done.7 = f32[16,1,8,256]{3,0,2,1:T(8,128)S(1)} collective-permute-done((f32[16,1,8,256]{3,0,2,1:T(8,128)S(1)}, f32[16,1,8,256]{3,0,2,1:T(8,128)S(1)}, u32[]{:S(2)}, u32[]{:S(2)}) %collective-permute-start.7) | collective-permute-done | bytes 131104 | tf_op jit(solution)/shard_map/ppermute | solution.py:16
  221.9 2.0 collective-permute-start.9
  224.0 2.9 %collective-permute-done.8 = f32[16,1,8,256]{3,0,2,1:T(8,128)S(1)} collective-permute-done((f32[16,1,8,256]{3,0,2,1:T(8,128)S(1)}, f32[16,1,8,256]{3,0,2,1:T(8,128)S(1)}, u32[]{:S(2)}, u32[]{:S(2)}) %collective-permute-start.8) | collective-permute-done | bytes 131104 | tf_op jit(solution)/shard_map/ppermute | solution.py:17
  226.9 2.2 collective-permute-done.9
  (269 shorter events, 23.1 us)
Async XLA Ops:
  7.2 79.9 %all-gather.2.cloned.1.call-start = ((), (), s32[]{:S(2)}) async-start(), calls=%async_computation | async-start | bytes 6684672 | tf_op jit(solution)/shard_map/all_gather | solution.py:61
  8.2 21.5 %copy-start.17 = (f32[1,8,256]{2,1,0:T(8,128)S(1)}, f32[1,8,256]{2,1,0:T(8,128)}, u32[]{:S(2)}) copy-start(f32[1,8,256]{2,1,0:T(8,128)} %param.8) | copy-start | bytes 24580
  8.2 21.4 %copy-start.16 = (f32[10,1,8,256]{3,2,1,0:T(8,128)S(1)}, f32[10,1,8,256]{3,2,1,0:T(8,128)}, u32[]{:S(2)}) copy-start(f32[10,1,8,256]{3,2,1,0:T(8,128)} %param.9) | copy-start | bytes 245764
  8.2 21.8 %copy-start.95 = (s32[256,10]{0,1:T(8,128)S(1)}, s32[256,10]{0,1:T(8,128)}, u32[]{:S(2)}) copy-start(s32[256,10]{0,1:T(8,128)} %param.11) | copy-start | bytes 30724
  8.2 8.7 %collective-permute-start.1 = (f32[16,1,8,256]{3,0,2,1:T(8,128)S(1)}, f32[16,1,8,256]{3,0,2,1:T(8,128)S(1)}, u32[]{:S(2)}, u32[]{:S(2)}) collective-permute-start(f32[16,1,8,256]{3,0,2,1:T(8,128)S(1)} %copy.125), channel_id=1, source_target_pairs={{16,0},{32,16},{48,32},{64,48},{80,64},{96,80},{112,96},{128,112},... | collective-permute-start | bytes 393224 | tf_op jit(solution)/shard_map/ppermute | solution.py:17
  14.1 7.1 %collective-permute-start.3 = (f32[16,1,8,256]{3,0,2,1:T(8,128)S(1)}, f32[16,1,8,256]{3,0,2,1:T(8,128)S(1)}, u32[]{:S(2)}, u32[]{:S(2)}) collective-permute-start(f32[16,1,8,256]{3,0,2,1:T(8,128)S(1)} %copy.125), channel_id=1, source_target_pairs={{0,16},{16,32},{32,48},{48,64},{64,80},{80,96},{96,112},{112,128},... | collective-permute-start | bytes 393224 | tf_op jit(solution)/shard_map/ppermute | solution.py:16
  22.9 11.2 %collective-permute-start = (f32[11,1,8,256]{3,2,1,0:T(8,128)S(1)}, f32[11,1,8,256]{3,2,1,0:T(8,128)S(1)}, u32[]{:S(2)}, u32[]{:S(2)}) collective-permute-start(f32[11,1,8,256]{3,2,1,0:T(8,128)S(1)} %pad_maximum_fusion.1), channel_id=1, source_target_pairs={{16,0},{32,16},{48,32},{64,48},{80,64},{96,80},{112,96},{128,112},... | collective-permute-start | bytes 270344 | tf_op jit(solution)/shard_map/ppermute | solution.py:17
  23.2 11.7 %collective-permute-start.2 = (f32[11,1,8,256]{3,2,1,0:T(8,128)S(1)}, f32[11,1,8,256]{3,2,1,0:T(8,128)S(1)}, u32[]{:S(2)}, u32[]{:S(2)}) collective-permute-start(f32[11,1,8,256]{3,2,1,0:T(8,128)S(1)} %pad_maximum_fusion.1), channel_id=1, source_target_pairs={{0,16},{16,32},{32,48},{48,64},{64,80},{80,96},{96,112},{112,128},... | collective-permute-start | bytes 270344 | tf_op jit(solution)/shard_map/ppermute | solution.py:16
  30.0 4.2 %copy-start.29 = (f32[10,256]{1,0:T(8,128)}, f32[10,256]{1,0:T(8,128)S(1)}, u32[]{:S(2)}) copy-start(f32[10,256]{1,0:T(8,128)S(1)} %convert_bitcast_fusion) | copy-start | bytes 30724
  87.1 4.4 %copy-start.5 = (f32[256,3,8,256]{3,0,2,1:T(8,128)S(1)}, f32[256,3,8,256]{3,0,2,1:T(8,128)}, u32[]{:S(2)}) copy-start(f32[256,3,8,256]{3,0,2,1:T(8,128)} %all-gather.2.cloned.1.call-done) | copy-start | bytes 18874372
  94.5 5.5 %copy-start.46 = (f32[8,256]{1,0:T(8,128)S(1)}, f32[8,256]{1,0:T(8,128)}, u32[]{:S(2)}) copy-start(f32[8,256]{1,0:T(8,128)} %get-tuple-element.44) | copy-start | bytes 24580
  94.5 5.5 %copy-start.47 = (f32[8,256]{1,0:T(8,128)S(1)}, f32[8,256]{1,0:T(8,128)}, u32[]{:S(2)}) copy-start(f32[8,256]{1,0:T(8,128)} %get-tuple-element.46) | copy-start | bytes 24580
  94.5 5.5 %copy-start.50 = (f32[8,256]{1,0:T(8,128)S(1)}, f32[8,256]{1,0:T(8,128)}, u32[]{:S(2)}) copy-start(f32[8,256]{1,0:T(8,128)} %get-tuple-element.104) | copy-start | bytes 24580
  94.5 5.5 %copy-start.51 = (f32[8,256]{1,0:T(8,128)S(1)}, f32[8,256]{1,0:T(8,128)}, u32[]{:S(2)}) copy-start(f32[8,256]{1,0:T(8,128)} %get-tuple-element.112) | copy-start | bytes 24580
  94.5 5.5 %copy-start.66 = (f32[8,256]{1,0:T(8,128)S(1)}, f32[8,256]{1,0:T(8,128)}, u32[]{:S(2)}) copy-start(f32[8,256]{1,0:T(8,128)} %get-tuple-element.114) | copy-start | bytes 24580
  94.5 5.5 %copy-start.69 = (f32[8,256]{1,0:T(8,128)S(1)}, f32[8,256]{1,0:T(8,128)}, u32[]{:S(2)}) copy-start(f32[8,256]{1,0:T(8,128)} %get-tuple-element.120) | copy-start | bytes 24580
  94.5 5.5 %copy-start.77 = (f32[8,256]{1,0:T(8,128)S(1)}, f32[8,256]{1,0:T(8,128)}, u32[]{:S(2)}) copy-start(f32[8,256]{1,0:T(8,128)} %get-tuple-element.91) | copy-start | bytes 24580
  94.5 5.5 %copy-start.78 = (f32[8,256]{1,0:T(8,128)S(1)}, f32[8,256]{1,0:T(8,128)}, u32[]{:S(2)}) copy-start(f32[8,256]{1,0:T(8,128)} %get-tuple-element.92) | copy-start | bytes 24580
  94.5 5.5 %copy-start.79 = (f32[8,256]{1,0:T(8,128)S(1)}, f32[8,256]{1,0:T(8,128)}, u32[]{:S(2)}) copy-start(f32[8,256]{1,0:T(8,128)} %get-tuple-element.93) | copy-start | bytes 24580
  94.5 5.5 %copy-start.80 = (f32[8,256]{1,0:T(8,128)S(1)}, f32[8,256]{1,0:T(8,128)}, u32[]{:S(2)}) copy-start(f32[8,256]{1,0:T(8,128)} %get-tuple-element.94) | copy-start | bytes 24580
  94.5 5.5 %copy-start.87 = (f32[8,256]{1,0:T(8,128)S(1)}, f32[8,256]{1,0:T(8,128)}, u32[]{:S(2)}) copy-start(f32[8,256]{1,0:T(8,128)} %get-tuple-element.35) | copy-start | bytes 24580
  94.5 5.5 %copy-start.88 = (f32[8,256]{1,0:T(8,128)S(1)}, f32[8,256]{1,0:T(8,128)}, u32[]{:S(2)}) copy-start(f32[8,256]{1,0:T(8,128)} %get-tuple-element.37) | copy-start | bytes 24580
  99.9 4.5 %copy-start = (f32[256,1,8,256]{3,0,2,1:T(8,128)}, f32[256,1,8,256]{3,0,2,1:T(8,128)S(1)}, u32[]{:S(2)}) copy-start(f32[256,1,8,256]{3,0,2,1:T(8,128)S(1)} %get-tuple-element.14) | copy-start | bytes 6291460
  99.9 4.5 %copy-start.1 = (f32[256,1,8,256]{3,0,2,1:T(8,128)}, f32[256,1,8,256]{3,0,2,1:T(8,128)S(1)}, u32[]{:S(2)}) copy-start(f32[256,1,8,256]{3,0,2,1:T(8,128)S(1)} %get-tuple-element.15) | copy-start | bytes 6291460
  99.9 4.5 %copy-start.2 = (f32[256,1,8,256]{3,0,2,1:T(8,128)}, f32[256,1,8,256]{3,0,2,1:T(8,128)S(1)}, u32[]{:S(2)}) copy-start(f32[256,1,8,256]{3,0,2,1:T(8,128)S(1)} %get-tuple-element.16) | copy-start | bytes 6291460
  99.9 4.5 %copy-start.3 = (f32[256,1,8,256]{3,0,2,1:T(8,128)}, f32[256,1,8,256]{3,0,2,1:T(8,128)S(1)}, u32[]{:S(2)}) copy-start(f32[256,1,8,256]{3,0,2,1:T(8,128)S(1)} %get-tuple-element.17) | copy-start | bytes 6291460
  99.9 5.1 %copy-start.4 = (f32[256,1,8,256]{3,0,2,1:T(8,128)}, f32[256,1,8,256]{3,0,2,1:T(8,128)S(1)}, u32[]{:S(2)}) copy-start(f32[256,1,8,256]{3,0,2,1:T(8,128)S(1)} %get-tuple-element.18) | copy-start | bytes 6291460
  105.1 3.2 %copy-start.44 = (f32[8,256]{1,0:T(8,128)S(1)}, f32[8,256]{1,0:T(8,128)}, u32[]{:S(2)}) copy-start(f32[8,256]{1,0:T(8,128)} %get-tuple-element.47) | copy-start | bytes 24580
  105.1 3.2 %copy-start.45 = (f32[8,256]{1,0:T(8,128)S(1)}, f32[8,256]{1,0:T(8,128)}, u32[]{:S(2)}) copy-start(f32[8,256]{1,0:T(8,128)} %get-tuple-element.48) | copy-start | bytes 24580
  105.1 3.2 %copy-start.57 = (f32[8,256]{1,0:T(8,128)S(1)}, f32[8,256]{1,0:T(8,128)}, u32[]{:S(2)}) copy-start(f32[8,256]{1,0:T(8,128)} %get-tuple-element.132) | copy-start | bytes 24580
  105.1 3.2 %copy-start.58 = (f32[8,256]{1,0:T(8,128)S(1)}, f32[8,256]{1,0:T(8,128)}, u32[]{:S(2)}) copy-start(f32[8,256]{1,0:T(8,128)} %get-tuple-element.133) | copy-start | bytes 24580
  105.1 3.2 %copy-start.59 = (f32[8,256]{1,0:T(8,128)S(1)}, f32[8,256]{1,0:T(8,128)}, u32[]{:S(2)}) copy-start(f32[8,256]{1,0:T(8,128)} %get-tuple-element.134) | copy-start | bytes 24580
  105.1 3.2 %copy-start.60 = (f32[8,256]{1,0:T(8,128)S(1)}, f32[8,256]{1,0:T(8,128)}, u32[]{:S(2)}) copy-start(f32[8,256]{1,0:T(8,128)} %get-tuple-element.135) | copy-start | bytes 24580
  105.1 3.2 %copy-start.70 = (f32[8,256]{1,0:T(8,128)S(1)}, f32[8,256]{1,0:T(8,128)}, u32[]{:S(2)}) copy-start(f32[8,256]{1,0:T(8,128)} %get-tuple-element.126) | copy-start | bytes 24580
  105.1 3.2 %copy-start.71 = (f32[8,256]{1,0:T(8,128)S(1)}, f32[8,256]{1,0:T(8,128)}, u32[]{:S(2)}) copy-start(f32[8,256]{1,0:T(8,128)} %get-tuple-element.129) | copy-start | bytes 24580
  105.1 3.2 %copy-start.72 = (f32[8,256]{1,0:T(8,128)S(1)}, f32[8,256]{1,0:T(8,128)}, u32[]{:S(2)}) copy-start(f32[8,256]{1,0:T(8,128)} %get-tuple-element.130) | copy-start | bytes 24580
  105.1 3.2 %copy-start.73 = (f32[8,256]{1,0:T(8,128)S(1)}, f32[8,256]{1,0:T(8,128)}, u32[]{:S(2)}) copy-start(f32[8,256]{1,0:T(8,128)} %get-tuple-element.131) | copy-start | bytes 24580
  105.2 3.2 %copy-start.85 = (f32[8,256]{1,0:T(8,128)S(1)}, f32[8,256]{1,0:T(8,128)}, u32[]{:S(2)}) copy-start(f32[8,256]{1,0:T(8,128)} %get-tuple-element.38) | copy-start | bytes 24580
  105.2 3.2 %copy-start.86 = (f32[8,256]{1,0:T(8,128)S(1)}, f32[8,256]{1,0:T(8,128)}, u32[]{:S(2)}) copy-start(f32[8,256]{1,0:T(8,128)} %get-tuple-element.39) | copy-start | bytes 24580
  124.6 3.1 %copy-start.34 = (f32[8,256]{1,0:T(8,128)S(1)}, f32[8,256]{1,0:T(8,128)}, u32[]{:S(2)}) copy-start(f32[8,256]{1,0:T(8,128)} %get-tuple-element.51) | copy-start | bytes 24580
  124.6 3.1 %copy-start.35 = (f32[8,256]{1,0:T(8,128)S(1)}, f32[8,256]{1,0:T(8,128)}, u32[]{:S(2)}) copy-start(f32[8,256]{1,0:T(8,128)} %get-tuple-element.52) | copy-start | bytes 24580
  160.1 3.2 %copy-start.14 = (f32[256,1,8,256]{0,3,2,1:T(8,128)S(1)}, f32[256,1,8,256]{0,3,2,1:T(8,128)}, u32[]{:S(2)}) copy-start(f32[256,1,8,256]{0,3,2,1:T(8,128)} %copy.135) | copy-start | bytes 6291460
  202.0 7.5 %collective-permute-start.4 = (f32[16,1,8,256]{3,0,2,1:T(8,128)S(1)}, f32[16,1,8,256]{3,0,2,1:T(8,128)S(1)}, u32[]{:S(2)}, u32[]{:S(2)}) collective-permute-start(f32[16,1,8,256]{3,0,2,1:T(8,128)S(1)} %get-tuple-element.232), channel_id=1, source_target_pairs={{16,0},{32,16},{48,32},{64,48},{80,64},{96,80},{112,96},{128,112},... | collective-permute-start | bytes 393224 | tf_op jit(solution)/shard_map/ppermute | solution.py:17
  206.3 7.5 %collective-permute-start.5 = (f32[16,1,8,256]{3,0,2,1:T(8,128)S(1)}, f32[16,1,8,256]{3,0,2,1:T(8,128)S(1)}, u32[]{:S(2)}, u32[]{:S(2)}) collective-permute-start(f32[16,1,8,256]{3,0,2,1:T(8,128)S(1)} %get-tuple-element.232), channel_id=1, source_target_pairs={{0,16},{16,32},{32,48},{48,64},{64,80},{80,96},{96,112},{112,128},... | collective-permute-start | bytes 393224 | tf_op jit(solution)/shard_map/ppermute | solution.py:16
  214.1 5.0 %collective-permute-start.6 = (f32[16,1,8,256]{3,0,2,1:T(8,128)S(1)}, f32[16,1,8,256]{3,0,2,1:T(8,128)S(1)}, u32[]{:S(2)}, u32[]{:S(2)}) collective-permute-start(f32[16,1,8,256]{3,0,2,1:T(8,128)S(1)} %get-tuple-element.10), channel_id=1, source_target_pairs={{16,0},{32,16},{48,32},{64,48},{80,64},{96,80},{112,96},{128,112},... | collective-permute-start | bytes 393224 | tf_op jit(solution)/shard_map/ppermute | solution.py:17
  214.4 7.1 %collective-permute-start.7 = (f32[16,1,8,256]{3,0,2,1:T(8,128)S(1)}, f32[16,1,8,256]{3,0,2,1:T(8,128)S(1)}, u32[]{:S(2)}, u32[]{:S(2)}) collective-permute-start(f32[16,1,8,256]{3,0,2,1:T(8,128)S(1)} %get-tuple-element.10), channel_id=1, source_target_pairs={{0,16},{16,32},{32,48},{48,64},{64,80},{80,96},{96,112},{112,128},... | collective-permute-start | bytes 393224 | tf_op jit(solution)/shard_map/ppermute | solution.py:16
  221.8 5.0 %collective-permute-start.8 = (f32[16,1,8,256]{3,0,2,1:T(8,128)S(1)}, f32[16,1,8,256]{3,0,2,1:T(8,128)S(1)}, u32[]{:S(2)}, u32[]{:S(2)}) collective-permute-start(f32[16,1,8,256]{3,0,2,1:T(8,128)S(1)} %get-tuple-element.8), channel_id=1, source_target_pairs={{16,0},{32,16},{48,32},{64,48},{80,64},{96,80},{112,96},{128,112},... | collective-permute-start | bytes 393224 | tf_op jit(solution)/shard_map/ppermute | solution.py:17
  221.9 7.2 %collective-permute-start.9 = (f32[16,1,8,256]{3,0,2,1:T(8,128)S(1)}, f32[16,1,8,256]{3,0,2,1:T(8,128)S(1)}, u32[]{:S(2)}, u32[]{:S(2)}) collective-permute-start(f32[16,1,8,256]{3,0,2,1:T(8,128)S(1)} %get-tuple-element.8), channel_id=1, source_target_pairs={{0,16},{16,32},{32,48},{48,64},{64,80},{80,96},{96,112},{112,128},... | collective-permute-start | bytes 393224 | tf_op jit(solution)/shard_map/ppermute | solution.py:16
  (59 other events, 139.2 us)
Sparse Core Ops, SparseCore 0:
  22.1 64.9 all-gather.1
where the time goes:
time: 238 us; the launch traced here: 237 us
  waiting for transfers between devices  69.2 us (29%)
  local copies, waits for them, and re-layouts  65.9 us (28%)
  other arithmetic  49.8 us (21%)
  matrix products  20.3 us (9%)
  starting transfers between devices  16.5 us (7%)
  between operations  15.2 us (6%)
    all_gather x1, waiting for transfers between devices, shards(): piece = lax.all_gather(padded_solution, 'ma', axis=0, tiled=True)  45.2 us
    add x6, other arithmetic, diffuse(): total + 0.5 * (center + jnp.roll(center, offset, which_dim)) * (values -...  36 us
    add x10, local copies, waits for them, and re-layouts, diffuse(): total + 0.5 * (center + jnp.roll(center, offset, which_dim)) * (values -...  26.6 us
    unnamed x204, local copies, waits for them, and re-layouts  24.9 us
    dot_general x1, matrix products, shards(): jnp.einsum('kij,kjc->ic', g_rows, terms, precision=lax.Precision.HIGHEST)  20.3 us
    ppermute x5, waiting for transfers between devices, extended(): before = lax.ppermute(last, axis, up)  13.2 us
    ppermute x5, starting transfers between devices, extended(): after = lax.ppermute(initial, axis, down)  10.9 us
    ppermute x5, waiting for transfers between devices, extended(): after = lax.ppermute(initial, axis, down)  10.8 us
  transfers between devices with their start and end apart: 11, of which 9 were waited for; matrix products, arithmetic and copies ran while one was open for 8% of the time, Pallas kernels for 0%

commit v1 on v0

--- a/solution.py
+++ b/solution.py
@@ -58,7 +58,9 @@
     kl_pad = padded_fields[1:]
     padded_solution = extended(solution, (("gx", 1),), 1)
     image = solution + diffuse(mean_pad, padded_solution)
-    piece = lax.all_gather(padded_solution, "ma", axis=0, tiled=True)
+    piece = jnp.concatenate(
+        lax.all_to_all(jnp.stack([padded_solution] * lax.axis_size("ma")), "ma", 0, 0), axis=0
+    )
     count = piece.shape[0]
     terms = jnp.stack([diffuse(kl_pad[field_id], piece) for field_id in range(fields)])
     terms = terms.reshape(fields, count, cells)

time: 238 us -> 256 us (1.076)
  waiting for transfers between devices: 69.2 us -> 84.3 us
  between operations: 15.2 us -> 1.95 us
  local copies, waits for them, and re-layouts: 65.9 us -> 77.2 us
  starting transfers between devices: 16.5 us -> 25.5 us
  other arithmetic: 49.8 us -> 45.5 us
    all_to_all x0 -> x1, waiting for transfers between devices: none -> 67.9 us  [shards(): lax.all_to_all(jnp.stack([padded_solution] * lax.axis_size('ma')), 'ma',...]
    all_gather x1 -> x0, waiting for transfers between devices: 45.2 us -> none  [shards(): piece = lax.all_gather(padded_solution, 'ma', axis=0, tiled=True)]
    another operation x1 -> x11, local copies, waits for them, and re-layouts: 1.5 us -> 28.3 us  [shards(): jnp.stack([diffuse(kl_pad[field_id], piece) for field_id in range(fields)])]
    add x10 -> x0, local copies, waits for them, and re-layouts: 26.6 us -> none  [diffuse(): total + 0.5 * (center + jnp.roll(center, offset, which_dim)) * (values -...]
    all_to_all x0 -> x1, starting transfers between devices: none -> 6.49 us  [shards(): lax.all_to_all(jnp.stack([padded_solution] * lax.axis_size('ma')), 'ma',...]
    ppermute x5, waiting for transfers between devices: 13.2 us -> 8.96 us  [extended(): before = lax.ppermute(last, axis, up)]
    ppermute x5, starting transfers between devices: 10.9 us -> 15 us  [extended(): after = lax.ppermute(initial, axis, down)]
    ppermute x5, waiting for transfers between devices: 10.8 us -> 7.4 us  [extended(): after = lax.ppermute(initial, axis, down)]
  transfers between devices with their start and end apart: 11 -> 11, of which waited for: 9 -> 7; matrix products, arithmetic and copies ran while one was open for 8% -> 8% of each run, Pallas kernels for 0% -> 0%
where the time goes in v1:
time: 256 us; the launch traced here: 255 us
  waiting for transfers between devices  84.3 us (33%)
  local copies, waits for them, and re-layouts  77.2 us (30%)
  other arithmetic  45.5 us (18%)
  starting transfers between devices  25.5 us (10%)
  matrix products  20.3 us (8%)
    all_to_all x1, waiting for transfers between devices, shards(): lax.all_to_all(jnp.stack([padded_solution] * lax.axis_size('ma')), 'ma',...  67.9 us
    add x6, other arithmetic, diffuse(): total + 0.5 * (center + jnp.roll(center, offset, which_dim)) * (values -...  33.7 us
    another operation x11, local copies, waits for them, and re-layouts, shards(): jnp.stack([diffuse(kl_pad[field_id], piece) for field_id in range(fields)])  28.3 us
    unnamed x204, local copies, waits for them, and re-layouts  25.6 us
    dot_general x1, matrix products, shards(): jnp.einsum('kij,kjc->ic', g_rows, terms, precision=lax.Precision.HIGHEST)  20.3 us
    ppermute x5, starting transfers between devices, extended(): after = lax.ppermute(initial, axis, down)  15 us
    slice x20, local copies, waits for them, and re-layouts, diffuse(): jnp.roll(values, offset, which_dim)  13.6 us
    ppermute x5, waiting for transfers between devices, extended(): before = lax.ppermute(last, axis, up)  8.96 us
  transfers between devices with their start and end apart: 11, of which 7 were waited for; matrix products, arithmetic and copies ran while one was open for 8% of the time, Pallas kernels for 0%

profile of v1, /device:TPU:2, one launch (start us, length us, event | category | flops | bytes accessed | tf_op | source)
XLA Modules:
  0.0 254.7 jit_solution(9514024273658457474)
XLA Ops:
  1.6 5.8 %collective-permute-start = (f32[11,1,8,256]{3,2,1,0:T(8,128)S(1)}, f32[11,1,8,256]{3,2,1,0:T(8,128)S(1)}, u32[]{:S(2)}, u32[]{:S(2)}) collective-permute-start(f32[11,1,8,256]{3,2,1,0:T(8,128)S(1)} %pad_maximum_fusion.1), channel_id=1, source_target_pairs={{16,0},{32,16},{48,32},{64,48},{80,64},{96,80},{112,96},{128,112},... | collective-permute-start | bytes 270344 | tf_op jit(solution)/shard_map/ppermute | solution.py:17
  7.4 0.9 copy.173
  8.3 4.2 %collective-permute-start.1 = (f32[16,1,8,256]{3,0,2,1:T(8,128)S(1)}, f32[16,1,8,256]{3,0,2,1:T(8,128)S(1)}, u32[]{:S(2)}, u32[]{:S(2)}) collective-permute-start(f32[16,1,8,256]{3,0,2,1:T(8,128)S(1)} %copy.173), channel_id=1, source_target_pairs={{16,0},{32,16},{48,32},{64,48},{80,64},{96,80},{112,96},{128,112},... | collective-permute-start | bytes 393224 | tf_op jit(solution)/shard_map/ppermute | solution.py:17
  19.4 2.7 %convert_reduce_fusion = f32[10,256,256]{2,1,0:T(8,128)} fusion(s32[10,256,2]{1,2,0:T(2,128)S(1)} %copy-done.94), kind=kLoop, calls=%fused_computation | loop fusion | flops 3276800 | bytes 2641920 | tf_op jit(solution)/shard_map/reduce_sum | solution.py:40
  25.8 3.3 %stack.24 = f32[16,16,3,8,256]{4,3,2,1,0:T(8,128)} broadcast(f32[16,3,8,256]{3,2,1,0:T(8,128)S(1)} %copy.175), dimensions={1,2,3,4} | broadcast | bytes 6684672 | tf_op jit(solution)/shard_map/stack | solution.py:62
  29.1 6.5 %all-to-all-start = ((f32[16,16,3,8,256]{4,3,2,1,0:T(8,128)}), f32[16,16,3,8,256]{4,3,2,1,0:T(8,128)}, u32[]{:S(2)}, u32[]{:S(2)}) async-start(f32[16,16,3,8,256]{4,3,2,1,0:T(8,128)} %stack.24), calls=%async_computation | async-start | bytes 12582912 | tf_op jit(solution)/shard_map/all_to_all | solution.py:62
  42.0 67.9 %all-to-all-done = f32[16,16,3,8,256]{4,3,2,1,0:T(8,128)} async-done(((f32[16,16,3,8,256]{4,3,2,1,0:T(8,128)}), f32[16,16,3,8,256]{4,3,2,1,0:T(8,128)}, u32[]{:S(2)}, u32[]{:S(2)}) %all-to-all-start) | async-done | bytes 6291488 | tf_op jit(solution)/shard_map/all_to_all | solution.py:62
  109.9 3.0 %fusion.185 = (f32[256,1,8,255]{3,2,1,0:T(8,128)S(1)}, f32[256,1,8,255]{3,2,1,0:T(8,128)S(1)}) fusion(f32[256,3,8,256]{3,2,1,0:T(8,128)} %bitcast.15), kind=kLoop, calls=%fused_computation.401 | loop fusion | bytes 8355840 | tf_op jit(solution)/shard_map/jit(_roll_static)/slice | solution.py:30
  112.9 2.6 %fusion.187 = (f32[256,1,7,256]{3,2,1,0:T(8,128)S(1)}, f32[256,1,7,256]{3,2,1,0:T(8,128)S(1)}) fusion(f32[256,3,8,256]{3,2,1,0:T(8,128)} %bitcast.15), kind=kLoop, calls=%fused_computation.403 | loop fusion | bytes 7340032 | tf_op jit(solution)/shard_map/jit(_roll_static)/slice | solution.py:30
  115.5 1.9 fusion.184
  117.5 2.7 %fusion.186 = (f32[256,1,1,256]{3,2,1,0:T(1,128)S(1)}, f32[256,1,1,256]{3,2,1,0:T(1,128)S(1)}) fusion(f32[256,3,8,256]{3,2,1,0:T(8,128)} %bitcast.15), kind=kLoop, calls=%fused_computation.402 | loop fusion | bytes 1048576 | tf_op jit(solution)/shard_map/jit(_roll_static)/slice | solution.py:30
  120.3 5.4 %multiply_add_fusion = (f32[256,1,8,256]{3,2,1,0:T(8,128)}, f32[256,1,8,256]{3,2,1,0:T(8,128)S(1)}, f32[256,1,8,256]{3,2,1,0:T(8,128)S(1)}, f32[256,1,8,256]{3,2...) fusion(f32[8,256]{1,0:T(8,128)S(1)} %copy-done.78, ...), kind=kLoop, calls=%fused_computation.8 | loop fusion | flops 11010048 | bytes 29409280 | tf_op jit(solution)/shard_map/add | solution.py:29
  125.9 3.5 %multiply_add_fusion.1 = (f32[256,1,8,256]{3,2,1,0:T(8,128)}, f32[256,1,8,256]{3,2,1,0:T(8,128)}) fusion(f32[256,1,8,256]{3,2,1,0:T(8,128)S(1)} %get-tuple-element.20, f32[256,1,8,256]{3,2,1,0:T(8,128)S(1)} %get-tuple-element.19, f32[256,1,8,256]{3,2,1,0:T(8,128)S(1)} %get-tuple-element.18, f32[256,1,8,256]{3,2,1,0:T(8,128)S(1)} %get-tuple-element.17, ...), kind=kLoop, calls=%fused_computation.9 | loop fusion | flops 11534336 | bytes 16875520 | tf_op jit(solution)/shard_map/add | solution.py:29
  131.2 3.1 %copy.218 = f32[256,1,8,256]{0,3,2,1:T(8,128)} copy(f32[256,1,8,256]{3,2,1,0:T(8,128)} %get-tuple-element.22) | data formatting | bytes 4194304 | tf_op jit(solution)/shard_map/stack | solution.py:65
  134.4 6.2 %multiply_add_fusion.3 = (f32[256,1,8,256]{3,2,1,0:T(8,128)}, f32[256,1,8,256]{3,2,1,0:T(8,128)}) fusion(f32[256,1,8,256]{3,2,1,0:T(8,128)} %copy-done.4, f32[256,1,8,256]{3,2,1,0:T(8,128)} %copy-done.3, f32[256,1,8,256]{3,2,1,0:T(8,128)} %copy-done.2, f32[256,1,8,256]{3,2,1,0:T(8,128)} %copy-done.1, f32[256,1,8,256]{3,2,1,0:T(8,128)} %copy-done, ...), kind=kLoop, calls=%fused_computation.11 | loop fusion | flops 11534336 | bytes 16875520 | tf_op jit(solution)/shard_map/add | solution.py:29
  140.7 3.0 %copy.216 = f32[256,1,8,256]{0,3,2,1:T(8,128)} copy(f32[256,1,8,256]{3,2,1,0:T(8,128)} %get-tuple-element.24) | data formatting | bytes 4194304 | tf_op jit(solution)/shard_map/stack | solution.py:65
  143.8 6.2 %multiply_add_fusion.5 = (f32[256,1,8,256]{3,2,1,0:T(8,128)}, f32[256,1,8,256]{3,2,1,0:T(8,128)}) fusion(f32[256,1,8,256]{3,2,1,0:T(8,128)} %copy-done.4, f32[256,1,8,256]{3,2,1,0:T(8,128)} %copy-done.3, f32[256,1,8,256]{3,2,1,0:T(8,128)} %copy-done.2, f32[256,1,8,256]{3,2,1,0:T(8,128)} %copy-done.1, f32[256,1,8,256]{3,2,1,0:T(8,128)} %copy-done, ...), kind=kLoop, calls=%fused_computation.13 | loop fusion | flops 11534336 | bytes 16875520 | tf_op jit(solution)/shard_map/add | solution.py:29
  150.1 3.0 %copy.214 = f32[256,1,8,256]{0,3,2,1:T(8,128)} copy(f32[256,1,8,256]{3,2,1,0:T(8,128)} %get-tuple-element.26) | data formatting | bytes 4194304 | tf_op jit(solution)/shard_map/stack | solution.py:65
  153.2 6.2 %multiply_add_fusion.7 = (f32[256,1,8,256]{3,2,1,0:T(8,128)}, f32[256,1,8,256]{3,2,1,0:T(8,128)}) fusion(f32[256,1,8,256]{3,2,1,0:T(8,128)} %copy-done.4, f32[256,1,8,256]{3,2,1,0:T(8,128)} %copy-done.3, f32[256,1,8,256]{3,2,1,0:T(8,128)} %copy-done.2, f32[256,1,8,256]{3,2,1,0:T(8,128)} %copy-done.1, f32[256,1,8,256]{3,2,1,0:T(8,128)} %copy-done, ...), kind=kLoop, calls=%fused_computation.15 | loop fusion | flops 11534336 | bytes 16875520 | tf_op jit(solution)/shard_map/add | solution.py:29
  159.5 3.0 %copy.212 = f32[256,1,8,256]{0,3,2,1:T(8,128)} copy(f32[256,1,8,256]{3,2,1,0:T(8,128)} %get-tuple-element.28) | data formatting | bytes 4194304 | tf_op jit(solution)/shard_map/stack | solution.py:65
  162.5 6.2 %multiply_add_fusion.9 = f32[256,1,8,256]{3,2,1,0:T(8,128)} fusion(f32[256,1,8,256]{3,2,1,0:T(8,128)} %copy-done.4, f32[256,1,8,256]{3,2,1,0:T(8,128)} %copy-done.3, f32[256,1,8,256]{3,2,1,0:T(8,128)} %copy-done.2, f32[256,1,8,256]{3,2,1,0:T(8,128)} %copy-done.1, f32[256,1,8,256]{3,2,1,0:T(8,128)} %copy-done, f32[256,1,8,256]{3,2,1,0:T(8,128)S(1)} %get-tuple-element.15, ...), kind=kLoop, calls=%fused_computation.17 | loop fusion | flops 5767168 | bytes 14729216 | tf_op jit(solution)/shard_map/add | solution.py:29
  168.7 1.9 copy.211
  170.7 1.5 constant_dynamic-update-slice_fusion.9
  172.1 3.0 %copy.213 = f32[256,1,8,256]{0,3,2,1:T(8,128)} copy(f32[256,1,8,256]{3,2,1,0:T(8,128)} %get-tuple-element.27) | data formatting | bytes 4194304 | tf_op jit(solution)/shard_map/stack | solution.py:65
  175.1 3.1 %copy.215 = f32[256,1,8,256]{0,3,2,1:T(8,128)} copy(f32[256,1,8,256]{3,2,1,0:T(8,128)} %get-tuple-element.25) | data formatting | bytes 4194304 | tf_op jit(solution)/shard_map/stack | solution.py:65
  178.1 1.8 copy.217
  180.0 3.1 %copy.219 = f32[256,1,8,256]{0,3,2,1:T(8,128)} copy(f32[256,1,8,256]{3,2,1,0:T(8,128)} %get-tuple-element.21) | data formatting | bytes 4194304 | tf_op jit(solution)/shard_map/stack | solution.py:65
  183.0 1.9 copy.220
  184.9 3.2 %constant_dynamic-update-slice_fusion.8 = f32[10,256,2048]{1,2,0:T(8,128)} fusion(f32[10,256,2048]{1,2,0:T(8,128)} %constant_dynamic-update-slice_fusion.9, f32[1,256,2048]{1,2,0:T(8,128)} %bitcast.366), kind=kLoop, calls=%fused_computation.102 | loop fusion | bytes 4194304
  188.1 1.5 constant_dynamic-update-slice_fusion.7
  190.5 1.5 constant_dynamic-update-slice_fusion.6
  192.8 1.5 constant_dynamic-update-slice_fusion.5
  195.2 1.4 constant_dynamic-update-slice_fusion.4
  196.6 0.9 copy-done.11
  197.5 1.4 constant_dynamic-update-slice_fusion.3
  199.9 1.5 constant_dynamic-update-slice_fusion.2
  202.2 1.5 constant_dynamic-update-slice_fusion.1
  204.7 1.5 constant_dynamic-update-slice_fusion
  206.3 20.3 %broadcast_multiply_fusion = (f32[16,1,8,256]{3,0,2,1:T(8,128)S(1)}, f32[16,1,8,256]{3,0,2,1:T(8,128)S(1)}) fusion(f32[8,256,256,10]{2,1,0,3:T(8,128)} %bitcast.362, f32[10,256,256]{2,1,0:T(8,128)} %convert_reduce_fusion, s32[]{:T(128)S(6)} %select_n.3, f32[16,256]{1,0:T(8,128)S(1)} %copy-done.30, f32[10,256]{1,0:T(8,128)S(1)} %copy-done.29, ...), kind=kOutput, calls=%fused_computation.93 | convolution fusion | flops 1007575040 | bytes 22522500 | tf_op jit(solution)/shard_map/kij,kjc->ic/dot_general | solution.py:67
  226.8 4.8 %collective-permute-start.4 = (f32[16,1,8,256]{3,0,2,1:T(8,128)S(1)}, f32[16,1,8,256]{3,0,2,1:T(8,128)S(1)}, u32[]{:S(2)}, u32[]{:S(2)}) collective-permute-start(f32[16,1,8,256]{3,0,2,1:T(8,128)S(1)} %get-tuple-element.234), channel_id=1, source_target_pairs={{16,0},{32,16},{48,32},{64,48},{80,64},{96,80},{112,96},{128,112},... | collective-permute-start | bytes 393224 | tf_op jit(solution)/shard_map/ppermute | solution.py:17
  232.4 1.7 collective-permute-done.4
  234.1 4.6 %collective-permute-done.5 = f32[16,1,8,256]{3,0,2,1:T(8,128)S(1)} collective-permute-done((f32[16,1,8,256]{3,0,2,1:T(8,128)S(1)}, f32[16,1,8,256]{3,0,2,1:T(8,128)S(1)}, u32[]{:S(2)}, u32[]{:S(2)}) %collective-permute-start.5) | collective-permute-done | bytes 131104 | tf_op jit(solution)/shard_map/ppermute | solution.py:16
  239.1 2.0 collective-permute-start.7
  241.2 2.9 %collective-permute-done.6 = f32[16,1,8,256]{3,0,2,1:T(8,128)S(1)} collective-permute-done((f32[16,1,8,256]{3,0,2,1:T(8,128)S(1)}, f32[16,1,8,256]{3,0,2,1:T(8,128)S(1)}, u32[]{:S(2)}, u32[]{:S(2)}) %collective-permute-start.6) | collective-permute-done | bytes 131104 | tf_op jit(solution)/shard_map/ppermute | solution.py:17
  244.0 2.2 collective-permute-done.7
  246.6 2.0 collective-permute-start.9
  248.7 2.9 %collective-permute-done.8 = f32[16,1,8,256]{3,0,2,1:T(8,128)S(1)} collective-permute-done((f32[16,1,8,256]{3,0,2,1:T(8,128)S(1)}, f32[16,1,8,256]{3,0,2,1:T(8,128)S(1)}, u32[]{:S(2)}, u32[]{:S(2)}) %collective-permute-start.8) | collective-permute-done | bytes 131104 | tf_op jit(solution)/shard_map/ppermute | solution.py:17
  251.6 2.2 collective-permute-done.9
  (270 shorter events, 27.8 us)
Async XLA Ops:
  0.6 18.8 %copy-start.95 = (s32[256,10]{0,1:T(8,128)S(1)}, s32[256,10]{0,1:T(8,128)}, u32[]{:S(2)}) copy-start(s32[256,10]{0,1:T(8,128)} %param.11) | copy-start | bytes 30724
  0.6 18.8 %copy-start.94 = (s32[10,256,2]{1,2,0:T(2,128)S(1)}, s32[10,256,2]{1,2,0:T(2,128)}, u32[]{:S(2)}) copy-start(s32[10,256,2]{1,2,0:T(2,128)} %param.10) | copy-start | bytes 61444
  1.6 22.6 %collective-permute-start = (f32[11,1,8,256]{3,2,1,0:T(8,128)S(1)}, f32[11,1,8,256]{3,2,1,0:T(8,128)S(1)}, u32[]{:S(2)}, u32[]{:S(2)}) collective-permute-start(f32[11,1,8,256]{3,2,1,0:T(8,128)S(1)} %pad_maximum_fusion.1), channel_id=1, source_target_pairs={{16,0},{32,16},{48,32},{64,48},{80,64},{96,80},{112,96},{128,112},... | collective-permute-start | bytes 270344 | tf_op jit(solution)/shard_map/ppermute | solution.py:17
  7.4 17.5 %collective-permute-start.2 = (f32[11,1,8,256]{3,2,1,0:T(8,128)S(1)}, f32[11,1,8,256]{3,2,1,0:T(8,128)S(1)}, u32[]{:S(2)}, u32[]{:S(2)}) collective-permute-start(f32[11,1,8,256]{3,2,1,0:T(8,128)S(1)} %pad_maximum_fusion.1), channel_id=1, source_target_pairs={{0,16},{16,32},{32,48},{48,64},{64,80},{80,96},{96,112},{112,128},... | collective-permute-start | bytes 270344 | tf_op jit(solution)/shard_map/ppermute | solution.py:16
  8.3 17.2 %collective-permute-start.1 = (f32[16,1,8,256]{3,0,2,1:T(8,128)S(1)}, f32[16,1,8,256]{3,0,2,1:T(8,128)S(1)}, u32[]{:S(2)}, u32[]{:S(2)}) collective-permute-start(f32[16,1,8,256]{3,0,2,1:T(8,128)S(1)} %copy.173), channel_id=1, source_target_pairs={{16,0},{32,16},{48,32},{64,48},{80,64},{96,80},{112,96},{128,112},... | collective-permute-start | bytes 393224 | tf_op jit(solution)/shard_map/ppermute | solution.py:17
  12.5 13.0 %collective-permute-start.3 = (f32[16,1,8,256]{3,0,2,1:T(8,128)S(1)}, f32[16,1,8,256]{3,0,2,1:T(8,128)S(1)}, u32[]{:S(2)}, u32[]{:S(2)}) collective-permute-start(f32[16,1,8,256]{3,0,2,1:T(8,128)S(1)} %copy.173), channel_id=1, source_target_pairs={{0,16},{16,32},{32,48},{48,64},{64,80},{80,96},{96,112},{112,128},... | collective-permute-start | bytes 393224 | tf_op jit(solution)/shard_map/ppermute | solution.py:16
  16.6 6.2 %copy-start.16 = (f32[1,8,256]{2,1,0:T(8,128)S(1)}, f32[1,8,256]{2,1,0:T(8,128)}, u32[]{:S(2)}) copy-start(f32[1,8,256]{2,1,0:T(8,128)} %param.8) | copy-start | bytes 24580
  16.6 7.5 %copy-start.15 = (f32[10,1,8,256]{3,2,1,0:T(8,128)S(1)}, f32[10,1,8,256]{3,2,1,0:T(8,128)}, u32[]{:S(2)}) copy-start(f32[10,1,8,256]{3,2,1,0:T(8,128)} %param.9) | copy-start | bytes 245764
  19.4 6.4 %copy-start.28 = (f32[10,256]{1,0:T(8,128)}, f32[10,256]{1,0:T(8,128)S(1)}, u32[]{:S(2)}) copy-start(f32[10,256]{1,0:T(8,128)S(1)} %convert_bitcast_fusion) | copy-start | bytes 30724
  29.1 80.8 %all-to-all-start = ((f32[16,16,3,8,256]{4,3,2,1,0:T(8,128)}), f32[16,16,3,8,256]{4,3,2,1,0:T(8,128)}, u32[]{:S(2)}, u32[]{:S(2)}) async-start(f32[16,16,3,8,256]{4,3,2,1,0:T(8,128)} %stack.24), calls=%async_computation | async-start | bytes 12582912 | tf_op jit(solution)/shard_map/all_to_all | solution.py:62
  115.5 4.7 %copy-start.47 = (f32[8,256]{1,0:T(8,128)S(1)}, f32[8,256]{1,0:T(8,128)}, u32[]{:S(2)}) copy-start(f32[8,256]{1,0:T(8,128)} %get-tuple-element.47) | copy-start | bytes 24580
  115.5 4.7 %copy-start.66 = (f32[8,256]{1,0:T(8,128)S(1)}, f32[8,256]{1,0:T(8,128)}, u32[]{:S(2)}) copy-start(f32[8,256]{1,0:T(8,128)} %get-tuple-element.138) | copy-start | bytes 24580
  115.5 4.7 %copy-start.67 = (f32[8,256]{1,0:T(8,128)S(1)}, f32[8,256]{1,0:T(8,128)}, u32[]{:S(2)}) copy-start(f32[8,256]{1,0:T(8,128)} %get-tuple-element.139) | copy-start | bytes 24580
  115.5 4.7 %copy-start.77 = (f32[8,256]{1,0:T(8,128)S(1)}, f32[8,256]{1,0:T(8,128)}, u32[]{:S(2)}) copy-start(f32[8,256]{1,0:T(8,128)} %get-tuple-element.140) | copy-start | bytes 24580
  115.5 4.7 %copy-start.78 = (f32[8,256]{1,0:T(8,128)S(1)}, f32[8,256]{1,0:T(8,128)}, u32[]{:S(2)}) copy-start(f32[8,256]{1,0:T(8,128)} %get-tuple-element.141) | copy-start | bytes 24580
  115.5 4.7 %copy-start.93 = (f32[8,256]{1,0:T(8,128)S(1)}, f32[8,256]{1,0:T(8,128)}, u32[]{:S(2)}) copy-start(f32[8,256]{1,0:T(8,128)} %get-tuple-element.38) | copy-start | bytes 24580
  120.2 5.5 %copy-start.45 = (f32[8,256]{1,0:T(8,128)S(1)}, f32[8,256]{1,0:T(8,128)}, u32[]{:S(2)}) copy-start(f32[8,256]{1,0:T(8,128)} %get-tuple-element.46) | copy-start | bytes 24580
  120.2 5.5 %copy-start.46 = (f32[8,256]{1,0:T(8,128)S(1)}, f32[8,256]{1,0:T(8,128)}, u32[]{:S(2)}) copy-start(f32[8,256]{1,0:T(8,128)} %get-tuple-element.48) | copy-start | bytes 24580
  120.2 5.5 %copy-start.50 = (f32[8,256]{1,0:T(8,128)S(1)}, f32[8,256]{1,0:T(8,128)}, u32[]{:S(2)}) copy-start(f32[8,256]{1,0:T(8,128)} %get-tuple-element.106) | copy-start | bytes 24580
  120.3 5.5 %copy-start.51 = (f32[8,256]{1,0:T(8,128)S(1)}, f32[8,256]{1,0:T(8,128)}, u32[]{:S(2)}) copy-start(f32[8,256]{1,0:T(8,128)} %get-tuple-element.114) | copy-start | bytes 24580
  120.3 5.5 %copy-start.68 = (f32[8,256]{1,0:T(8,128)S(1)}, f32[8,256]{1,0:T(8,128)}, u32[]{:S(2)}) copy-start(f32[8,256]{1,0:T(8,128)} %get-tuple-element.116) | copy-start | bytes 24580
  120.3 5.5 %copy-start.71 = (f32[8,256]{1,0:T(8,128)S(1)}, f32[8,256]{1,0:T(8,128)}, u32[]{:S(2)}) copy-start(f32[8,256]{1,0:T(8,128)} %get-tuple-element.122) | copy-start | bytes 24580
  120.3 5.5 %copy-start.81 = (f32[8,256]{1,0:T(8,128)S(1)}, f32[8,256]{1,0:T(8,128)}, u32[]{:S(2)}) copy-start(f32[8,256]{1,0:T(8,128)} %get-tuple-element.93) | copy-start | bytes 24580
  120.3 5.5 %copy-start.82 = (f32[8,256]{1,0:T(8,128)S(1)}, f32[8,256]{1,0:T(8,128)}, u32[]{:S(2)}) copy-start(f32[8,256]{1,0:T(8,128)} %get-tuple-element.94) | copy-start | bytes 24580
  120.3 5.5 %copy-start.83 = (f32[8,256]{1,0:T(8,128)S(1)}, f32[8,256]{1,0:T(8,128)}, u32[]{:S(2)}) copy-start(f32[8,256]{1,0:T(8,128)} %get-tuple-element.95) | copy-start | bytes 24580
  120.3 5.5 %copy-start.84 = (f32[8,256]{1,0:T(8,128)S(1)}, f32[8,256]{1,0:T(8,128)}, u32[]{:S(2)}) copy-start(f32[8,256]{1,0:T(8,128)} %get-tuple-element.96) | copy-start | bytes 24580
  120.3 5.5 %copy-start.91 = (f32[8,256]{1,0:T(8,128)S(1)}, f32[8,256]{1,0:T(8,128)}, u32[]{:S(2)}) copy-start(f32[8,256]{1,0:T(8,128)} %get-tuple-element.37) | copy-start | bytes 24580
  120.3 5.5 %copy-start.92 = (f32[8,256]{1,0:T(8,128)S(1)}, f32[8,256]{1,0:T(8,128)}, u32[]{:S(2)}) copy-start(f32[8,256]{1,0:T(8,128)} %get-tuple-element.39) | copy-start | bytes 24580
  125.7 3.6 %copy-start = (f32[256,1,8,256]{3,2,1,0:T(8,128)}, f32[256,1,8,256]{3,2,1,0:T(8,128)S(1)}, u32[]{:S(2)}) copy-start(f32[256,1,8,256]{3,2,1,0:T(8,128)S(1)} %get-tuple-element.16) | copy-start | bytes 6291460
  125.7 3.6 %copy-start.1 = (f32[256,1,8,256]{3,2,1,0:T(8,128)}, f32[256,1,8,256]{3,2,1,0:T(8,128)S(1)}, u32[]{:S(2)}) copy-start(f32[256,1,8,256]{3,2,1,0:T(8,128)S(1)} %get-tuple-element.17) | copy-start | bytes 6291460
  125.7 3.9 %copy-start.2 = (f32[256,1,8,256]{3,2,1,0:T(8,128)}, f32[256,1,8,256]{3,2,1,0:T(8,128)S(1)}, u32[]{:S(2)}) copy-start(f32[256,1,8,256]{3,2,1,0:T(8,128)S(1)} %get-tuple-element.18) | copy-start | bytes 6291460
  125.7 4.6 %copy-start.3 = (f32[256,1,8,256]{3,2,1,0:T(8,128)}, f32[256,1,8,256]{3,2,1,0:T(8,128)S(1)}, u32[]{:S(2)}) copy-start(f32[256,1,8,256]{3,2,1,0:T(8,128)S(1)} %get-tuple-element.19) | copy-start | bytes 6291460
  125.8 5.3 %copy-start.4 = (f32[256,1,8,256]{3,2,1,0:T(8,128)}, f32[256,1,8,256]{3,2,1,0:T(8,128)S(1)}, u32[]{:S(2)}) copy-start(f32[256,1,8,256]{3,2,1,0:T(8,128)S(1)} %get-tuple-element.20) | copy-start | bytes 6291460
  131.1 3.2 %copy-start.59 = (f32[8,256]{1,0:T(8,128)S(1)}, f32[8,256]{1,0:T(8,128)}, u32[]{:S(2)}) copy-start(f32[8,256]{1,0:T(8,128)} %get-tuple-element.136) | copy-start | bytes 24580
  131.1 3.2 %copy-start.60 = (f32[8,256]{1,0:T(8,128)S(1)}, f32[8,256]{1,0:T(8,128)}, u32[]{:S(2)}) copy-start(f32[8,256]{1,0:T(8,128)} %get-tuple-element.137) | copy-start | bytes 24580
  131.1 3.2 %copy-start.72 = (f32[8,256]{1,0:T(8,128)S(1)}, f32[8,256]{1,0:T(8,128)}, u32[]{:S(2)}) copy-start(f32[8,256]{1,0:T(8,128)} %get-tuple-element.128) | copy-start | bytes 24580
  131.1 3.2 %copy-start.73 = (f32[8,256]{1,0:T(8,128)S(1)}, f32[8,256]{1,0:T(8,128)}, u32[]{:S(2)}) copy-start(f32[8,256]{1,0:T(8,128)} %get-tuple-element.131) | copy-start | bytes 24580
  131.1 3.2 %copy-start.74 = (f32[8,256]{1,0:T(8,128)S(1)}, f32[8,256]{1,0:T(8,128)}, u32[]{:S(2)}) copy-start(f32[8,256]{1,0:T(8,128)} %get-tuple-element.132) | copy-start | bytes 24580
  131.1 3.2 %copy-start.75 = (f32[8,256]{1,0:T(8,128)S(1)}, f32[8,256]{1,0:T(8,128)}, u32[]{:S(2)}) copy-start(f32[8,256]{1,0:T(8,128)} %get-tuple-element.133) | copy-start | bytes 24580
  131.1 3.2 %copy-start.89 = (f32[8,256]{1,0:T(8,128)S(1)}, f32[8,256]{1,0:T(8,128)}, u32[]{:S(2)}) copy-start(f32[8,256]{1,0:T(8,128)} %get-tuple-element.40) | copy-start | bytes 24580
  131.1 3.2 %copy-start.90 = (f32[8,256]{1,0:T(8,128)S(1)}, f32[8,256]{1,0:T(8,128)}, u32[]{:S(2)}) copy-start(f32[8,256]{1,0:T(8,128)} %get-tuple-element.41) | copy-start | bytes 24580
  184.9 3.3 %copy-start.13 = (f32[256,1,8,256]{0,3,2,1:T(8,128)S(1)}, f32[256,1,8,256]{0,3,2,1:T(8,128)}, u32[]{:S(2)}) copy-start(f32[256,1,8,256]{0,3,2,1:T(8,128)} %copy.213) | copy-start | bytes 6291460
  226.8 7.3 %collective-permute-start.4 = (f32[16,1,8,256]{3,0,2,1:T(8,128)S(1)}, f32[16,1,8,256]{3,0,2,1:T(8,128)S(1)}, u32[]{:S(2)}, u32[]{:S(2)}) collective-permute-start(f32[16,1,8,256]{3,0,2,1:T(8,128)S(1)} %get-tuple-element.234), channel_id=1, source_target_pairs={{16,0},{32,16},{48,32},{64,48},{80,64},{96,80},{112,96},{128,112},... | collective-permute-start | bytes 393224 | tf_op jit(solution)/shard_map/ppermute | solution.py:17
  231.6 7.1 %collective-permute-start.5 = (f32[16,1,8,256]{3,0,2,1:T(8,128)S(1)}, f32[16,1,8,256]{3,0,2,1:T(8,128)S(1)}, u32[]{:S(2)}, u32[]{:S(2)}) collective-permute-start(f32[16,1,8,256]{3,0,2,1:T(8,128)S(1)} %get-tuple-element.234), channel_id=1, source_target_pairs={{0,16},{16,32},{32,48},{48,64},{64,80},{80,96},{96,112},{112,128},... | collective-permute-start | bytes 393224 | tf_op jit(solution)/shard_map/ppermute | solution.py:16
  239.0 5.0 %collective-permute-start.6 = (f32[16,1,8,256]{3,0,2,1:T(8,128)S(1)}, f32[16,1,8,256]{3,0,2,1:T(8,128)S(1)}, u32[]{:S(2)}, u32[]{:S(2)}) collective-permute-start(f32[16,1,8,256]{3,0,2,1:T(8,128)S(1)} %get-tuple-element.12), channel_id=1, source_target_pairs={{16,0},{32,16},{48,32},{64,48},{80,64},{96,80},{112,96},{128,112},... | collective-permute-start | bytes 393224 | tf_op jit(solution)/shard_map/ppermute | solution.py:17
  239.1 7.2 %collective-permute-start.7 = (f32[16,1,8,256]{3,0,2,1:T(8,128)S(1)}, f32[16,1,8,256]{3,0,2,1:T(8,128)S(1)}, u32[]{:S(2)}, u32[]{:S(2)}) collective-permute-start(f32[16,1,8,256]{3,0,2,1:T(8,128)S(1)} %get-tuple-element.12), channel_id=1, source_target_pairs={{0,16},{16,32},{32,48},{48,64},{64,80},{80,96},{96,112},{112,128},... | collective-permute-start | bytes 393224 | tf_op jit(solution)/shard_map/ppermute | solution.py:16
  246.5 5.0 %collective-permute-start.8 = (f32[16,1,8,256]{3,0,2,1:T(8,128)S(1)}, f32[16,1,8,256]{3,0,2,1:T(8,128)S(1)}, u32[]{:S(2)}, u32[]{:S(2)}) collective-permute-start(f32[16,1,8,256]{3,0,2,1:T(8,128)S(1)} %get-tuple-element.10), channel_id=1, source_target_pairs={{16,0},{32,16},{48,32},{64,48},{80,64},{96,80},{112,96},{128,112},... | collective-permute-start | bytes 393224 | tf_op jit(solution)/shard_map/ppermute | solution.py:17
  246.6 7.2 %collective-permute-start.9 = (f32[16,1,8,256]{3,0,2,1:T(8,128)S(1)}, f32[16,1,8,256]{3,0,2,1:T(8,128)S(1)}, u32[]{:S(2)}, u32[]{:S(2)}) collective-permute-start(f32[16,1,8,256]{3,0,2,1:T(8,128)S(1)} %get-tuple-element.10), channel_id=1, source_target_pairs={{0,16},{16,32},{32,48},{48,64},{64,80},{80,96},{96,112},{112,128},... | collective-permute-start | bytes 393224 | tf_op jit(solution)/shard_map/ppermute | solution.py:16
  (59 other events, 154.1 us)
